TPU v7x, 256 devices: a whole 4x4x8 slice. The times are simulated.
256 devices in a mesh: section: 8 (over z_hi, core), fsdp: 4 (over x), tensor: 8 (over y, z_lo).
Axes of the slice: x: 4, y: 4, z: 8 (z_hi: 4, z_lo: 2; z = z_hi * 2 + z_lo), core: 2. Of those that a mesh axis runs over, the one named last changes fastest.
Arguments:
- hidden: bfloat16 [8, 512, 8192], P('section', 'fsdp', 'tensor'), may hold values from -16 to 16
- encoder_weight: bfloat16 [8, 1024, 8192], P('section', 'fsdp', 'tensor'), may hold values from -0.0625 to 0.0625
- decoder_weight: bfloat16 [8, 1024, 8192], P('section', 'fsdp', 'tensor'), may hold values from -16 to 16
- query_weight: bfloat16 [8, 8192, 8192], P('section', 'fsdp', 'tensor'), may hold values from -32 to 32
- key_weight: bfloat16 [8, 8192, 1024], P('section', 'fsdp', 'tensor'), may hold values from -1 to 1
- value_weight: bfloat16 [8, 8192, 1024], P('section', 'fsdp', 'tensor'), may hold values from -0.0625 to 0.0625
- segments: int32 [8, 4, 128], P('section', 'fsdp'), may hold values from 0 to 3, never falling along the last dimension, each value on 1 to 64 neighbouring positions
- out_grad: bfloat16 [8, 512, 8192], P('section', 'fsdp', 'tensor'), may hold values from -6 to 6
Outputs:
- attention: bfloat16 [8, 512, 8192], P('section', 'fsdp', 'tensor')
- hidden_grad: bfloat16 [8, 512, 8192], P('section', 'fsdp', 'tensor')
- encoder_grad: float32 [8, 1024, 8192], P('section', 'fsdp', 'tensor')
- decoder_grad: float32 [8, 1024, 8192], P('section', 'fsdp', 'tensor')
Inputs may be any that keep to these rules, and one draw needn't show every extreme that they name: `segments`: segment ids never fall along a row, and attention stays inside one document of one row; each document spans at most 64 tokens, and some document spans exactly that many.
All inputs are finite; a program needn't handle non-finite values.
Results may differ from a plain program's by a relative error of at most 0.025.
Values may be sent and summed in bfloat16 or wider, within the bound.
No kernel may reach another device: no remote copies, remote signals or barrier semaphores. Data moves between devices by JAX's collectives and lax.ppermute only.
A program may use at most 128 MiB of HBM per device.

v0:
```python
import math
import jax
import jax.numpy as jnp
from jax import lax
from jax.sharding import PartitionSpec as P

D = 8192
DH = 128
NORM_EPS = 1e-05
ROPE_BASE = 500000.0
NEG_FILL = -1e30


def passed_along(value, axis, steps):
    count = lax.axis_size(axis)
    pairs = [(source, (source + steps) % count) for source in range(count)]
    return lax.ppermute(value, axis, pairs)


def rope_tables(segment_row, dim):
    length = segment_row.shape[0]
    positions = jnp.arange(length, dtype=jnp.int32)
    earlier = jnp.sum((segment_row[None, :] < segment_row[:, None]).astype(jnp.int32), axis=1)
    places = (positions - earlier).astype(jnp.float32)
    frequency = jnp.exp(jnp.arange(0, dim, 2).astype(jnp.float32) * (-math.log(ROPE_BASE) / dim))
    angles = places[:, None] * frequency[None, :]
    allowed = (segment_row[None, :] == segment_row[:, None]) & (
        positions[None, :] <= positions[:, None]
    )
    return (jnp.cos(angles), jnp.sin(angles), allowed)


def rotate(values, cosine, sine):
    half_dim = values.shape[-1] // 2
    first_half = values[..., :half_dim]
    second_half = values[..., half_dim:]
    cosine_rows = cosine[:, None, :]
    sine_rows = sine[:, None, :]
    return jnp.concatenate(
        [
            first_half * cosine_rows - second_half * sine_rows,
            second_half * cosine_rows + first_half * sine_rows,
        ],
        axis=-1,
    )


def unrotate(grads, cosine, sine):
    half_dim = grads.shape[-1] // 2
    first_half = grads[..., :half_dim]
    second_half = grads[..., half_dim:]
    cosine_rows = cosine[:, None, :]
    sine_rows = sine[:, None, :]
    return jnp.concatenate(
        [
            first_half * cosine_rows + second_half * sine_rows,
            second_half * cosine_rows - first_half * sine_rows,
        ],
        axis=-1,
    )


def product(form, left, right):
    return jnp.einsum(form, left, right, preferred_element_type=jnp.float32)


def attend(queries, keys_in, values_in, upstream, segment_row, head_count, pair_count):
    length = queries.shape[0]
    group_size = head_count // pair_count
    cosine, sine, allowed = rope_tables(segment_row, DH)
    query_rot = (
        rotate(queries.reshape(length, head_count, DH), cosine, sine)
        .astype(jnp.bfloat16)
        .reshape(length, pair_count, group_size, DH)
    )
    key_rot = rotate(keys_in.reshape(length, pair_count, DH), cosine, sine).astype(jnp.bfloat16)
    value_heads = values_in.reshape(length, pair_count, DH).astype(jnp.bfloat16)
    factor = 1.0 / math.sqrt(DH)
    scores = product("tkgd,skd->kgts", query_rot, key_rot) * factor
    scores = jnp.where(allowed, scores, NEG_FILL)
    row_max = jnp.max(scores, axis=-1, keepdims=True)
    exponent = jnp.exp(scores - row_max)
    probs = exponent / jnp.sum(exponent, axis=-1, keepdims=True)
    probs_low = probs.astype(jnp.bfloat16)
    mixed = product("kgts,skd->tkgd", probs_low, value_heads).reshape(length, head_count * DH)
    cot_heads = upstream.reshape(length, pair_count, group_size, DH)
    prob_grad = product("tkgd,skd->kgts", cot_heads, value_heads)
    value_grad = product("kgts,tkgd->skd", probs_low, cot_heads)
    score_grad = probs * (prob_grad - jnp.sum(probs * prob_grad, axis=-1, keepdims=True))
    score_grad_low = score_grad.astype(jnp.bfloat16)
    query_grad = product("kgts,skd->tkgd", score_grad_low, key_rot) * factor
    key_grad = product("kgts,tkgd->skd", score_grad_low, query_rot) * factor
    query_grad = unrotate(query_grad.reshape(length, head_count, DH), cosine, sine).reshape(
        length, head_count * DH
    )
    key_grad = unrotate(key_grad, cosine, sine).reshape(length, pair_count * DH)
    return (
        mixed.astype(jnp.bfloat16),
        query_grad.astype(jnp.bfloat16),
        key_grad.astype(jnp.bfloat16),
        value_grad.reshape(length, pair_count * DH).astype(jnp.bfloat16),
    )


def row_total(values):
    return lax.psum(values, "tensor")


def token_sum(left, right):
    return lax.psum_scatter(
        lax.dot_general(
            left, right, (((0,), (0,)), ((), ())), preferred_element_type=jnp.float32
        ).astype(jnp.bfloat16),
        "fsdp",
        scatter_dimension=0,
        tiled=True,
    ).astype(jnp.float32)


def body(
    hidden,
    encoder_weight,
    decoder_weight,
    query_weight,
    key_weight,
    value_weight,
    segments,
    out_grad,
):
    residual = hidden[0]
    segment_row = segments[0, 0]
    upstream = out_grad[0]
    contract_last = (((1,), (1,)), ((), ()))
    encoder_rows, decoder_rows = (
        lax.all_gather(encoder_weight[0], "fsdp", axis=0, tiled=True),
        lax.all_gather(decoder_weight[0], "fsdp", axis=0, tiled=True),
    )
    code_partial = lax.dot_general(
        residual, encoder_rows, contract_last, preferred_element_type=jnp.float32
    )
    code_sent = lax.psum(code_partial, "tensor").astype(jnp.bfloat16)
    code_received = passed_along(code_sent, "section", 1)
    decoded = jnp.dot(code_received, decoder_rows, preferred_element_type=jnp.float32)
    norm_factor = lax.rsqrt(row_total(jnp.sum(decoded * decoded, axis=1)) / D + NORM_EPS)[:, None]
    normed = (decoded * norm_factor).astype(jnp.bfloat16)
    normed_full = lax.all_gather(normed, "tensor", axis=1, tiled=True)
    query_width = query_weight.shape[2]
    key_width = key_weight.shape[2]
    query_rows, key_rows, value_rows = (
        lax.all_gather(query_weight[0], "fsdp", axis=0, tiled=True),
        lax.all_gather(key_weight[0], "fsdp", axis=0, tiled=True),
        lax.all_gather(value_weight[0], "fsdp", axis=0, tiled=True),
    )
    queries = jnp.dot(normed_full, query_rows, preferred_element_type=jnp.float32)
    keys_all = jnp.dot(normed_full, key_rows, preferred_element_type=jnp.float32)
    values_all = jnp.dot(normed_full, value_rows, preferred_element_type=jnp.float32)
    mixed, query_grad, key_grad, value_grad = attend(
        queries, keys_all, values_all, upstream, segment_row, query_width // DH, key_width // DH
    )
    total = lax.dot_general(
        query_rows, query_grad, contract_last, preferred_element_type=jnp.float32
    )
    total = total + lax.dot_general(
        key_rows, key_grad, contract_last, preferred_element_type=jnp.float32
    )
    total = total + lax.dot_general(
        value_rows, value_grad, contract_last, preferred_element_type=jnp.float32
    )
    normed_grad = (
        lax.psum_scatter(total.astype(jnp.bfloat16), "tensor", scatter_dimension=0, tiled=True)
        .astype(jnp.float32)
        .T
    )
    inner_dot = row_total(jnp.sum(normed_grad * decoded, axis=1))[:, None]
    decoded_grad = (norm_factor * normed_grad - decoded * norm_factor**3 * inner_dot / D).astype(
        jnp.bfloat16
    )
    decoder_grad = token_sum(code_received, decoded_grad)
    code_grad_partial = lax.dot_general(
        decoded_grad, decoder_rows, contract_last, preferred_element_type=jnp.float32
    )
    code_grad_sent = lax.psum(code_grad_partial.astype(jnp.bfloat16), "tensor")
    code_grad = passed_along(code_grad_sent, "section", -1)
    encoder_grad = token_sum(code_grad, residual)
    hidden_grad = jnp.dot(code_grad, encoder_rows, preferred_element_type=jnp.float32).astype(
        jnp.bfloat16
    )
    return (mixed[None], hidden_grad[None], encoder_grad[None], decoder_grad[None])


def solution(mesh):
    placed = (
        P("section", "fsdp", "tensor"),
        P("section", "fsdp", "tensor"),
        P("section", "fsdp", "tensor"),
        P("section", "fsdp", "tensor"),
        P("section", "fsdp", "tensor"),
        P("section", "fsdp", "tensor"),
        P("section", "fsdp", None),
        P("section", "fsdp", "tensor"),
    )
    return jax.shard_map(
        body,
        mesh=mesh,
        in_specs=placed,
        out_specs=(
            P("section", "fsdp", "tensor"),
            P("section", "fsdp", "tensor"),
            P("section", "fsdp", "tensor"),
            P("section", "fsdp", "tensor"),
        ),
        check_vma=False,
    )
```

profile of v0, /device:TPU:1, one launch (start us, length us, event | category | flops | bytes accessed | tf_op | source)
XLA Modules:
  0.0 637.2 jit_solution(18349268483296418803)
XLA Ops:
  7.2 0.7 all-gather.14.cloned.1.call-update
  8.0 0.7 all-gather.16.cloned.1.call-update
  8.7 0.7 all-gather.20.cloned.1.call-update
  9.4 37.3 %all-gather.14.cloned.1.call-done = bf16[1,1024,1024]{2,1,0:T(8,128)(2,1)} async-done(((bf16[1,256,1024]{2,1,0:T(8,128)(2,1)}), bf16[1,1024,1024]{2,1,0:T(8,128)(2,1)}) %all-gather.14.cloned.1.call-update) | async-done | bytes 2097168 | tf_op jit(solution)/shard_map/all_gather | solution.py:135
  46.8 2.4 fusion.18
  49.2 38.5 %all-reduce.4 = bf16[128,1024]{1,0:T(8,128)(2,1)S(1)} all-reduce(f32[128,1024]{1,0:T(8,128)S(1)} %fusion.18), channel_id=1, replica_groups=mesh['section'=8,'fsdp'=4,'tensor'=8] {'tensor'}, use_global_device_ids=true, to_apply=%region_0.0 | all-reduce | flops 131072 | bytes 786432 | tf_op jit(solution)/shard_map/psum | solution.py:141
  87.7 8.9 %collective-permute-start = (bf16[128,1024]{1,0:T(8,128)(2,1)S(1)}, bf16[128,1024]{1,0:T(8,128)(2,1)S(1)}, u32[]{:S(2)}, u32[]{:S(2)}) collective-permute-start(bf16[128,1024]{1,0:T(8,128)(2,1)S(1)} %all-reduce.4), channel_id=1, source_target_pairs={{0,32},{32,64},{64,96},{96,128},{128,160},{160,192},{192,224},{224... | collective-permute-start | bytes 786440 | tf_op jit(solution)/shard_map/ppermute | solution.py:17
  96.6 4.6 collective-permute-done
  101.2 2.2 multiply_reduce_fusion.1
  103.5 15.4 %psum.29 = f32[128]{0:T(128)S(1)} all-reduce(f32[128]{0:T(128)S(1)} %get-tuple-element.26), channel_id=1, replica_groups=mesh['section'=8,'fsdp'=4,'tensor'=8] {'tensor'}, use_global_device_ids=true, to_apply=%region_2.0 | all-reduce | flops 128 | bytes 1024 | tf_op jit(solution)/shard_map/psum | solution.py:106
  118.9 0.5 multiply_multiply_fusion
  119.4 0.8 multiply_convert_fusion.1
  120.3 0.5 all-gather.18.cloned.1.call-update
  120.9 0.5 all-gather.22.cloned.1.call-update
  121.4 0.2 reduce-scatter.4.cloned.1.call-start
  121.7 0.1 copy-done.7
  121.8 0.8 copy.47
  122.6 0.1 convert_reduce_fusion
  122.7 0.7 fusion.64
  123.4 0.3 multiply_cosine_fusion
  123.7 52.0 %all-gather.12.cloned.1.call-done = bf16[128,8192]{1,0:T(8,128)(2,1)} async-done(((bf16[128,1024]{1,0:T(8,128)(2,1)}), bf16[128,8192]{1,0:T(8,128)(2,1)}) %all-gather.12.cloned.1.call-update) | async-done | bytes 2097168 | tf_op jit(solution)/shard_map/all_gather | solution.py:146
  175.7 3.3 fusion.35
  179.0 0.8 fusion.84
  179.8 30.6 %all-gather.18.cloned.1.call-done = bf16[1,8192,128]{2,1,0:T(8,128)(2,1)} async-done(((bf16[1,2048,128]{2,1,0:T(8,128)(2,1)}), bf16[1,8192,128]{2,1,0:T(8,128)(2,1)}) %all-gather.18.cloned.1.call-update) | async-done | bytes 2097168 | tf_op jit(solution)/shard_map/all_gather | solution.py:152
  210.4 2.9 fusion.44
  213.3 155.4 %all-gather.22.cloned.1.call-done = bf16[1,8192,1024]{2,1,0:T(8,128)(2,1)} async-done(((bf16[1,2048,1024]{2,1,0:T(8,128)(2,1)}), bf16[1,8192,1024]{2,1,0:T(8,128)(2,1)}) %all-gather.22.cloned.1.call-update) | async-done | bytes 16777232 | tf_op jit(solution)/shard_map/all_gather | solution.py:150
  368.7 8.1 %fusion.22 = f32[16,8,8,128]{3,1,2,0:T(8,128)S(1)} fusion(bf16[128,8192]{1,0:T(8,128)(2,1)S(1)} %copy-done.1, bf16[1,8192,1024]{2,1,0:T(8,128)(2,1)} %all-gather.22.cloned.1.call-done), kind=kOutput, calls=%fused_computation.29 | convolution fusion | flops 2147483648 | bytes 19398656 | tf_op jit(solution)/shard_map/dot_general | solution.py:154
  376.8 0.1 copy.46
  377.0 0.2 fusion.94
  377.2 0.2 subtract_convert_fusion.1
  377.4 0.3 copy-done.8
  377.7 0.3 fusion.95
  378.0 0.1 fusion.51
  378.1 0.2 multiply_reduce_fusion
  378.4 0.1 fusion.52
  378.6 0.1 copy-done.9
  378.6 0.4 fusion.39
  379.0 0.3 fusion.20
  379.3 0.8 fusion.78
  380.1 0.2 add_convert_fusion
  380.4 0.1 pad_maximum_fusion.1
  380.5 0.9 copy.31
  381.4 13.7 %fusion = f32[128,8192]{1,0:T(8,128)} fusion(bf16[128,1024]{0,1:T(8,128)(2,1)} %bitcast.152, bf16[1,8192,1024]{2,1,0:T(8,128)(2,1)} %all-gather.22.cloned.1.call-done), kind=kOutput, calls=%fused_computation | convolution fusion | flops 2147483648 | bytes 21233664 | tf_op jit(solution)/shard_map/dot_general | solution.py:160
  395.1 4.9 convolution_add_fusion.1
  399.9 5.4 fusion.5
  405.4 0.0 all-reduce.3.cloned.1.call-start
  405.4 56.1 %reduce-scatter.4.cloned.1.call-done = bf16[1024,128]{0,1:T(8,128)(2,1)} async-done(((bf16[8192,128]{0,1:T(8,128)(2,1)}), bf16[1024,128]{0,1:T(8,128)(2,1)}) %reduce-scatter.4.cloned.1.call-update) | async-done | bytes 262160 | tf_op jit(solution)/shard_map/reduce_scatter | solution.py:170
  461.5 1.1 fusion.49
  462.6 13.3 %psum.30 = f32[128]{0:T(128)S(1)} all-reduce(f32[128]{0:T(128)S(1)} %fusion.49), channel_id=1, replica_groups=mesh['section'=8,'fsdp'=4,'tensor'=8] {'tensor'}, use_global_device_ids=true, to_apply=%region_9.10 | all-reduce | flops 128 | bytes 1024 | tf_op jit(solution)/shard_map/psum | solution.py:106
  475.9 2.5 fusion.28
  478.5 0.0 reduce-scatter.8.cloned.1.call-start
  478.5 3.2 convolution_convert_fusion
  481.8 73.3 %all-reduce.3.cloned.1.call-done = bf16[128,1024]{1,0:T(8,128)(2,1)} async-done(((bf16[128,1024]{1,0:T(8,128)(2,1)}), bf16[128,1024]{1,0:T(8,128)(2,1)}) %all-reduce.3.cloned.1.call-update) | async-done | bytes 262160 | tf_op jit(solution)/shard_map/psum | solution.py:182
  555.1 6.0 collective-permute-start.1
  561.1 7.7 %collective-permute-done.1 = bf16[128,1024]{1,0:T(8,128)(2,1)S(1)} collective-permute-done((bf16[128,1024]{1,0:T(8,128)(2,1)}, bf16[128,1024]{1,0:T(8,128)(2,1)S(1)}, u32[]{:S(2)}, u32[]{:S(2)}) %collective-permute-start.1) | collective-permute-done | bytes 262176 | tf_op jit(solution)/shard_map/ppermute | solution.py:17
  568.8 2.0 convolution_convert_fusion.1
  570.9 0.2 convolution_convert_fusion.2
  571.1 0.9 copy.34
  572.0 0.5 copy-done.3
  572.5 1.2 fusion.32
  573.7 20.1 %reduce-scatter.8.cloned.1.call-done = bf16[256,1024]{1,0:T(8,128)(2,1)} async-done(((bf16[1024,1024]{1,0:T(8,128)(2,1)}), bf16[256,1024]{1,0:T(8,128)(2,1)}) %reduce-scatter.8.cloned.1.call-update) | async-done | bytes 524304 | tf_op jit(solution)/shard_map/reduce_scatter | solution.py:110
  593.8 2.1 bitcast_convert_fusion
  596.0 32.3 %reduce-scatter.6.cloned.1.call-done = bf16[256,1024]{1,0:T(8,128)(2,1)} async-done(((bf16[1024,1024]{1,0:T(8,128)(2,1)}), bf16[256,1024]{1,0:T(8,128)(2,1)}) %reduce-scatter.6.cloned.1.call-update) | async-done | bytes 524304 | tf_op jit(solution)/shard_map/reduce_scatter | solution.py:110
  628.3 2.1 bitcast_convert_fusion.1
  (62 shorter events, 0.5 us)
Async XLA Ops:
  7.2 39.6 %copy-start = (bf16[1,128,1024]{2,1,0:T(8,128)(2,1)S(1)}, bf16[1,128,1024]{2,1,0:T(8,128)(2,1)}, u32[]{:S(2)}) copy-start(bf16[1,128,1024]{2,1,0:T(8,128)(2,1)} %param.8) | copy-start | bytes 786436
  7.2 39.6 %all-gather.14.cloned.1.call-start = ((), (), s32[]{:S(2)}) async-start(), calls=%async_computation.8 | async-start | bytes 2621440 | tf_op jit(solution)/shard_map/all_gather | solution.py:135
  7.9 88.7 %all-gather.16.cloned.1.call-start = ((), (), s32[]{:S(2)}) async-start(), calls=%async_computation.9 | async-start | bytes 2621440 | tf_op jit(solution)/shard_map/all_gather | solution.py:136
  8.7 115.0 %all-gather.20.cloned.1.call-start = ((), (), s32[]{:S(2)}) async-start(), calls=%async_computation.11 | async-start | bytes 2621440 | tf_op jit(solution)/shard_map/all_gather | solution.py:151
  9.4 166.3 %all-gather.12.cloned.1.call-start = ((), (), s32[]{:S(2)}) async-start(), calls=%async_computation.3 | async-start | bytes 2359296 | tf_op jit(solution)/shard_map/all_gather | solution.py:146
  87.7 13.6 %collective-permute-start = (bf16[128,1024]{1,0:T(8,128)(2,1)S(1)}, bf16[128,1024]{1,0:T(8,128)(2,1)S(1)}, u32[]{:S(2)}, u32[]{:S(2)}) collective-permute-start(bf16[128,1024]{1,0:T(8,128)(2,1)S(1)} %all-reduce.4), channel_id=1, source_target_pairs={{0,32},{32,64},{64,96},{96,128},{128,160},{160,192},{192,224},{224... | collective-permute-start | bytes 786440 | tf_op jit(solution)/shard_map/ppermute | solution.py:17
  101.2 19.6 %copy-start.5 = (bf16[128,1024]{1,0:T(8,128)(2,1)}, bf16[128,1024]{1,0:T(8,128)(2,1)S(1)}, u32[]{:S(2)}) copy-start(bf16[128,1024]{1,0:T(8,128)(2,1)S(1)} %collective-permute-done) | copy-start | bytes 786436
  119.4 0.9 copy-start.21
  120.2 90.2 %all-gather.18.cloned.1.call-start = ((), (), s32[]{:S(2)}) async-start(), calls=%async_computation.10 | async-start | bytes 2621440 | tf_op jit(solution)/shard_map/all_gather | solution.py:152
  120.8 1.0 copy-start.7
  120.8 1.7 copy-start.24
  120.9 247.9 %all-gather.22.cloned.1.call-start = ((), (), s32[]{:S(2)}) async-start(), calls=%async_computation.12 | async-start | bytes 20971520 | tf_op jit(solution)/shard_map/all_gather | solution.py:150
  121.4 340.1 %reduce-scatter.4.cloned.1.call-start = ((), (), s32[]{:S(2)}) async-start(), calls=%async_computation.4 | async-start | bytes 2359296 | tf_op jit(solution)/shard_map/reduce_scatter | solution.py:170
  122.5 56.5 %copy-start.17 = (f32[64]{0:T(128)}, f32[64]{0:T(128)S(1)}, u32[]{:S(2)}) copy-start(f32[64]{0:T(128)S(1)} %multiply_exponential_fusion) | copy-start | bytes 772
  122.7 56.4 %copy-start.19 = (f32[128]{0:T(128)}, f32[128]{0:T(128)S(1)}, u32[]{:S(2)}) copy-start(f32[128]{0:T(128)S(1)} %subtract_convert_fusion.2) | copy-start | bytes 1540
  175.7 34.7 %copy-start.1 = (bf16[128,8192]{1,0:T(8,128)(2,1)S(1)}, bf16[128,8192]{1,0:T(8,128)(2,1)}, u32[]{:S(2)}) copy-start(bf16[128,8192]{1,0:T(8,128)(2,1)} %all-gather.12.cloned.1.call-done) | copy-start | bytes 6291460
  376.9 0.7 copy-start.8
  376.9 0.7 copy-start.12
  377.2 1.0 copy-start.6
  377.2 1.0 copy-start.15
  378.0 0.6 copy-start.9
  378.1 0.9 copy-start.13
  378.4 0.9 copy-start.18
  378.4 0.9 copy-start.20
  381.4 13.7 %copy-start.2 = (bf16[1,8192,128]{2,1,0:T(8,128)(2,1)S(1)}, bf16[1,8192,128]{2,1,0:T(8,128)(2,1)}, u32[]{:S(2)}) copy-start(bf16[1,8192,128]{2,1,0:T(8,128)(2,1)} %all-gather.20.cloned.1.call-done) | copy-start | bytes 6291460
  381.4 13.7 %copy-start.11 = (bf16[128,1,64]{0,2,1:T(8,128)(2,1)S(1)}, bf16[128,1,64]{0,2,1:T(8,128)(2,1)}, u32[]{:S(2)}) copy-start(bf16[128,1,64]{0,2,1:T(8,128)(2,1)} %get-tuple-element.19) | copy-start | bytes 49156
  395.1 4.9 copy-start.10
  395.1 4.9 copy-start.14
  405.3 70.6 %copy-start.4 = (bf16[1,1024,1024]{2,1,0:T(8,128)(2,1)S(1)}, bf16[1,1024,1024]{2,1,0:T(8,128)(2,1)}, u32[]{:S(2)}) copy-start(bf16[1,1024,1024]{2,1,0:T(8,128)(2,1)} %all-gather.16.cloned.1.call-done) | copy-start | bytes 6291460
  405.3 70.6 %copy-start.22 = (f32[128]{0:T(128)S(1)}, f32[128]{0:T(128)}, u32[]{:S(2)}) copy-start(f32[128]{0:T(128)} %copy-done.21) | copy-start | bytes 1540
  405.3 70.6 %copy-start.23 = (f32[128]{0:T(128)S(1)}, f32[128]{0:T(128)}, u32[]{:S(2)}) copy-start(f32[128]{0:T(128)} %get-tuple-element.24) | copy-start | bytes 1540
  405.4 149.7 %all-reduce.3.cloned.1.call-start = ((), (), s32[]{:S(2)}) async-start(), calls=%async_computation.5 | async-start | bytes 524288 | tf_op jit(solution)/shard_map/psum | solution.py:182
  478.5 115.4 %reduce-scatter.8.cloned.1.call-start = ((), (), s32[]{:S(2)}) async-start(), calls=%async_computation.7 | async-start | bytes 2621440 | tf_op jit(solution)/shard_map/reduce_scatter | solution.py:110
  481.8 89.1 %copy-start.16 = (bf16[128,128,1]{1,0,2:T(8,128)(2,1)S(1)}, bf16[128,128,1]{1,0,2:T(8,128)(2,1)}, u32[]{:S(2)}) copy-start(bf16[128,128,1]{1,0,2:T(8,128)(2,1)} %fusion.44) | copy-start | bytes 98308
  481.8 146.5 %reduce-scatter.6.cloned.1.call-start = ((), (), s32[]{:S(2)}) async-start(), calls=%async_computation.6 | async-start | bytes 2621440 | tf_op jit(solution)/shard_map/reduce_scatter | solution.py:110
  555.1 13.7 %collective-permute-start.1 = (bf16[128,1024]{1,0:T(8,128)(2,1)}, bf16[128,1024]{1,0:T(8,128)(2,1)S(1)}, u32[]{:S(2)}, u32[]{:S(2)}) collective-permute-start(bf16[128,1024]{1,0:T(8,128)(2,1)} %all-reduce.3.cloned.1.call-done), channel_id=1, source_target_pairs={{0,224},{32,0},{64,32},{96,64},{128,96},{160,128},{192,160},{224,1... | collective-permute-start | bytes 786440 | tf_op jit(solution)/shard_map/ppermute | solution.py:17
  570.9 1.7 copy-start.3
Sparse Core Ops, SparseCore 0:
  9.8 36.9 all-gather.13
  48.6 33.3 all-gather.15
  83.8 33.3 all-gather.19
  120.4 55.3 all-gather.11
  177.4 32.9 all-gather.17
  212.1 156.6 all-gather.21
  405.5 55.9 reduce-scatter.3
  478.6 76.4 all-reduce.2
  557.7 36.1 reduce-scatter.7
  596.2 31.9 reduce-scatter.5
where the time goes:
time: 638 us; the launch traced here: 637 us
  waiting for transfers between devices  473 us (74%)
  blocking collectives  67.2 us (11%)
  matrix products  53.3 us (8%)
  starting transfers between devices  15.5 us (2%)
  between operations  14.5 us (2%)
  other arithmetic  10.2 us (2%)
    all_gather x1, waiting for transfers between devices, body(): lax.all_gather(query_weight[0], 'fsdp', axis=0, tiled=True)  155 us
    psum x1, waiting for transfers between devices, body(): code_grad_sent = lax.psum(code_grad_partial.astype(jnp.bfloat16), 'tensor')  73.3 us
    reduce_scatter x1, waiting for transfers between devices, body(): lax.psum_scatter(total.astype(jnp.bfloat16), 'tensor', scatter_dimension=...  56.1 us
    reduce_scatter x2, waiting for transfers between devices, token_sum(): lax.psum_scatter(lax.dot_general(left, right, (((0,), (0,)), ((), ())), p...  52.5 us
    all_gather x1, waiting for transfers between devices, body(): normed_full = lax.all_gather(normed, 'tensor', axis=1, tiled=True)  52 us
    psum x1, blocking collectives, body(): code_sent = lax.psum(code_partial, 'tensor').astype(jnp.bfloat16)  38.5 us
    all_gather x1, waiting for transfers between devices, body(): lax.all_gather(encoder_weight[0], 'fsdp', axis=0, tiled=True)  37.3 us
    all_gather x1, waiting for transfers between devices, body(): lax.all_gather(value_weight[0], 'fsdp', axis=0, tiled=True)  30.6 us
  transfers between devices with their start and end apart: 12, of which 10 were waited for; matrix products, arithmetic and copies ran while one was open for 4% of the time, Pallas kernels for 0%

commit v1 on v0

--- a/solution.py
+++ b/solution.py
@@ -179,7 +179,9 @@
     code_grad_partial = lax.dot_general(
         decoded_grad, decoder_rows, contract_last, preferred_element_type=jnp.float32
     )
-    code_grad_sent = lax.psum(code_grad_partial.astype(jnp.bfloat16), "tensor")
+    code_grad_sent = jnp.sum(
+        lax.all_gather(code_grad_partial.astype(jnp.bfloat16), "tensor"), axis=0
+    )
     code_grad = passed_along(code_grad_sent, "section", -1)
     encoder_grad = token_sum(code_grad, residual)
     hidden_grad = jnp.dot(code_grad, encoder_rows, preferred_element_type=jnp.float32).astype(

time: 638 us -> 614 us (0.962)
  waiting for transfers between devices: 473 us -> 451 us
    psum x1 -> x0, waiting for transfers between devices: 73.3 us -> none  [body(): code_grad_sent = lax.psum(code_grad_partial.astype(jnp.bfloat16), 'tensor')]
    all_gather x0 -> x1, waiting for transfers between devices: none -> 53.5 us  [body(): lax.all_gather(code_grad_partial.astype(jnp.bfloat16), 'tensor')]
where the time goes in v1:
time: 614 us; the launch traced here: 613 us
  waiting for transfers between devices  451 us (73%)
  blocking collectives  67.2 us (11%)
  matrix products  53.3 us (9%)
  between operations  14.5 us (2%)
  other arithmetic  12.2 us (2%)
  starting transfers between devices  11.1 us (2%)
    all_gather x1, waiting for transfers between devices, body(): lax.all_gather(query_weight[0], 'fsdp', axis=0, tiled=True)  155 us
    reduce_scatter x1, waiting for transfers between devices, body(): lax.psum_scatter(total.astype(jnp.bfloat16), 'tensor', scatter_dimension=...  56.1 us
    all_gather x1, waiting for transfers between devices, body(): lax.all_gather(code_grad_partial.astype(jnp.bfloat16), 'tensor')  53.5 us
    all_gather x1, waiting for transfers between devices, body(): normed_full = lax.all_gather(normed, 'tensor', axis=1, tiled=True)  52 us
    reduce_scatter x2, waiting for transfers between devices, token_sum(): lax.psum_scatter(lax.dot_general(left, right, (((0,), (0,)), ((), ())), p...  50.3 us
    psum x1, blocking collectives, body(): code_sent = lax.psum(code_partial, 'tensor').astype(jnp.bfloat16)  38.5 us
    all_gather x1, waiting for transfers between devices, body(): lax.all_gather(encoder_weight[0], 'fsdp', axis=0, tiled=True)  37.3 us
    all_gather x1, waiting for transfers between devices, body(): lax.all_gather(value_weight[0], 'fsdp', axis=0, tiled=True)  30.6 us
  transfers between devices with their start and end apart: 12, of which 10 were waited for; matrix products, arithmetic and copies ran while one was open for 4% of the time, Pallas kernels for 0%

profile of v1, /device:TPU:1, one launch (start us, length us, event | category | flops | bytes accessed | tf_op | source)
XLA Modules:
  0.0 613.4 jit_solution(14641273075411690784)
XLA Ops:
  7.2 0.7 all-gather.16.cloned.1.call-update
  8.0 0.7 all-gather.18.cloned.1.call-update
  8.7 0.7 all-gather.22.cloned.1.call-update
  9.4 37.3 %all-gather.16.cloned.1.call-done = bf16[1,1024,1024]{2,1,0:T(8,128)(2,1)} async-done(((bf16[1,256,1024]{2,1,0:T(8,128)(2,1)}), bf16[1,1024,1024]{2,1,0:T(8,128)(2,1)}) %all-gather.16.cloned.1.call-update) | async-done | bytes 2097168 | tf_op jit(solution)/shard_map/all_gather | solution.py:135
  46.8 2.4 fusion.18
  49.2 38.5 %all-reduce.1 = bf16[128,1024]{1,0:T(8,128)(2,1)S(1)} all-reduce(f32[128,1024]{1,0:T(8,128)S(1)} %fusion.18), channel_id=1, replica_groups=mesh['section'=8,'fsdp'=4,'tensor'=8] {'tensor'}, use_global_device_ids=true, to_apply=%region_0.0 | all-reduce | flops 131072 | bytes 786432 | tf_op jit(solution)/shard_map/psum | solution.py:141
  87.7 8.9 %collective-permute-start = (bf16[128,1024]{1,0:T(8,128)(2,1)S(1)}, bf16[128,1024]{1,0:T(8,128)(2,1)S(1)}, u32[]{:S(2)}, u32[]{:S(2)}) collective-permute-start(bf16[128,1024]{1,0:T(8,128)(2,1)S(1)} %all-reduce.1), channel_id=1, source_target_pairs={{0,32},{32,64},{64,96},{96,128},{128,160},{160,192},{192,224},{224... | collective-permute-start | bytes 786440 | tf_op jit(solution)/shard_map/ppermute | solution.py:17
  96.6 4.6 collective-permute-done
  101.2 2.2 multiply_reduce_fusion.1
  103.5 15.4 %psum.22 = f32[128]{0:T(128)S(1)} all-reduce(f32[128]{0:T(128)S(1)} %get-tuple-element.26), channel_id=1, replica_groups=mesh['section'=8,'fsdp'=4,'tensor'=8] {'tensor'}, use_global_device_ids=true, to_apply=%region_2.0 | all-reduce | flops 128 | bytes 1024 | tf_op jit(solution)/shard_map/psum | solution.py:106
  118.9 0.5 multiply_multiply_fusion
  119.4 0.8 multiply_convert_fusion.1
  120.3 0.5 all-gather.20.cloned.1.call-update
  120.9 0.5 all-gather.24.cloned.1.call-update
  121.4 0.2 reduce-scatter.4.cloned.1.call-start
  121.7 0.1 copy-done.7
  121.8 0.8 copy.47
  122.6 0.1 convert_reduce_fusion
  122.7 0.7 fusion.64
  123.4 0.3 multiply_cosine_fusion
  123.7 52.0 %all-gather.14.cloned.1.call-done = bf16[128,8192]{1,0:T(8,128)(2,1)} async-done(((bf16[128,1024]{1,0:T(8,128)(2,1)}), bf16[128,8192]{1,0:T(8,128)(2,1)}) %all-gather.14.cloned.1.call-update) | async-done | bytes 2097168 | tf_op jit(solution)/shard_map/all_gather | solution.py:146
  175.7 3.3 fusion.35
  179.0 0.8 fusion.84
  179.8 30.6 %all-gather.20.cloned.1.call-done = bf16[1,8192,128]{2,1,0:T(8,128)(2,1)} async-done(((bf16[1,2048,128]{2,1,0:T(8,128)(2,1)}), bf16[1,8192,128]{2,1,0:T(8,128)(2,1)}) %all-gather.20.cloned.1.call-update) | async-done | bytes 2097168 | tf_op jit(solution)/shard_map/all_gather | solution.py:152
  210.4 2.9 fusion.44
  213.3 155.4 %all-gather.24.cloned.1.call-done = bf16[1,8192,1024]{2,1,0:T(8,128)(2,1)} async-done(((bf16[1,2048,1024]{2,1,0:T(8,128)(2,1)}), bf16[1,8192,1024]{2,1,0:T(8,128)(2,1)}) %all-gather.24.cloned.1.call-update) | async-done | bytes 16777232 | tf_op jit(solution)/shard_map/all_gather | solution.py:150
  368.7 8.1 %fusion.22 = f32[16,8,8,128]{3,1,2,0:T(8,128)S(1)} fusion(bf16[128,8192]{1,0:T(8,128)(2,1)S(1)} %copy-done.1, bf16[1,8192,1024]{2,1,0:T(8,128)(2,1)} %all-gather.24.cloned.1.call-done), kind=kOutput, calls=%fused_computation.29 | convolution fusion | flops 2147483648 | bytes 19398656 | tf_op jit(solution)/shard_map/dot_general | solution.py:154
  376.8 0.1 copy.46
  377.0 0.2 fusion.94
  377.2 0.2 subtract_convert_fusion.1
  377.4 0.3 copy-done.8
  377.7 0.3 fusion.95
  378.0 0.1 fusion.51
  378.1 0.2 multiply_reduce_fusion
  378.4 0.1 fusion.52
  378.6 0.1 copy-done.9
  378.6 0.4 fusion.39
  379.0 0.3 fusion.20
  379.3 0.8 fusion.78
  380.1 0.2 add_convert_fusion
  380.4 0.1 pad_maximum_fusion.1
  380.5 0.9 copy.31
  381.4 13.7 %fusion = f32[128,8192]{1,0:T(8,128)} fusion(bf16[128,1024]{0,1:T(8,128)(2,1)} %bitcast.154, bf16[1,8192,1024]{2,1,0:T(8,128)(2,1)} %all-gather.24.cloned.1.call-done), kind=kOutput, calls=%fused_computation | convolution fusion | flops 2147483648 | bytes 21233664 | tf_op jit(solution)/shard_map/dot_general | solution.py:160
  395.1 4.9 convolution_add_fusion.1
  399.9 5.4 fusion.5
  405.4 56.1 %reduce-scatter.4.cloned.1.call-done = bf16[1024,128]{0,1:T(8,128)(2,1)} async-done(((bf16[8192,128]{0,1:T(8,128)(2,1)}), bf16[1024,128]{0,1:T(8,128)(2,1)}) %reduce-scatter.4.cloned.1.call-update) | async-done | bytes 262160 | tf_op jit(solution)/shard_map/reduce_scatter | solution.py:170
  461.5 1.1 fusion.49
  462.6 13.3 %psum.23 = f32[128]{0:T(128)S(1)} all-reduce(f32[128]{0:T(128)S(1)} %fusion.49), channel_id=1, replica_groups=mesh['section'=8,'fsdp'=4,'tensor'=8] {'tensor'}, use_global_device_ids=true, to_apply=%region_9.10 | all-reduce | flops 128 | bytes 1024 | tf_op jit(solution)/shard_map/psum | solution.py:106
  475.9 2.5 fusion.28
  478.5 0.0 reduce-scatter.8.cloned.1.call-start
  478.5 3.2 convolution_convert_fusion
  481.8 53.5 %all-gather.26.cloned.1.call-done = bf16[1024,1024]{1,0:T(8,128)(2,1)} async-done(((bf16[128,1024]{1,0:T(8,128)(2,1)}), bf16[1024,1024]{1,0:T(8,128)(2,1)}) %all-gather.26.cloned.1.call-update) | async-done | bytes 2097168 | tf_op jit(solution)/shard_map/all_gather | solution.py:183
  535.3 2.0 reduce_sum.62
  537.3 1.5 collective-permute-start.1
  538.9 8.1 %collective-permute-done.1 = bf16[128,1024]{1,0:T(8,128)(2,1)S(1)} collective-permute-done((bf16[128,1024]{1,0:T(8,128)(2,1)S(1)}, bf16[128,1024]{1,0:T(8,128)(2,1)S(1)}, u32[]{:S(2)}, u32[]{:S(2)}) %collective-permute-start.1) | collective-permute-done | bytes 262176 | tf_op jit(solution)/shard_map/ppermute | solution.py:17
  547.0 2.0 convolution_convert_fusion.1
  549.0 0.3 convolution_convert_fusion.2
  549.3 0.9 copy.34
  550.1 0.7 copy-done.3
  550.8 1.2 fusion.32
  552.0 18.0 %reduce-scatter.8.cloned.1.call-done = bf16[256,1024]{1,0:T(8,128)(2,1)} async-done(((bf16[1024,1024]{1,0:T(8,128)(2,1)}), bf16[256,1024]{1,0:T(8,128)(2,1)}) %reduce-scatter.8.cloned.1.call-update) | async-done | bytes 524304 | tf_op jit(solution)/shard_map/reduce_scatter | solution.py:110
  570.0 2.1 bitcast_convert_fusion
  572.1 32.3 %reduce-scatter.6.cloned.1.call-done = bf16[256,1024]{1,0:T(8,128)(2,1)} async-done(((bf16[1024,1024]{1,0:T(8,128)(2,1)}), bf16[256,1024]{1,0:T(8,128)(2,1)}) %reduce-scatter.6.cloned.1.call-update) | async-done | bytes 524304 | tf_op jit(solution)/shard_map/reduce_scatter | solution.py:110
  604.4 2.1 bitcast_convert_fusion.1
  (63 shorter events, 0.6 us)
Async XLA Ops:
  7.2 39.6 %copy-start = (bf16[1,128,1024]{2,1,0:T(8,128)(2,1)S(1)}, bf16[1,128,1024]{2,1,0:T(8,128)(2,1)}, u32[]{:S(2)}) copy-start(bf16[1,128,1024]{2,1,0:T(8,128)(2,1)} %param.8) | copy-start | bytes 786436
  7.2 39.6 %all-gather.16.cloned.1.call-start = ((), (), s32[]{:S(2)}) async-start(), calls=%async_computation.7 | async-start | bytes 2621440 | tf_op jit(solution)/shard_map/all_gather | solution.py:135
  7.9 88.7 %all-gather.18.cloned.1.call-start = ((), (), s32[]{:S(2)}) async-start(), calls=%async_computation.8 | async-start | bytes 2621440 | tf_op jit(solution)/shard_map/all_gather | solution.py:136
  8.7 115.0 %all-gather.22.cloned.1.call-start = ((), (), s32[]{:S(2)}) async-start(), calls=%async_computation.10 | async-start | bytes 2621440 | tf_op jit(solution)/shard_map/all_gather | solution.py:151
  9.4 166.3 %all-gather.14.cloned.1.call-start = ((), (), s32[]{:S(2)}) async-start(), calls=%async_computation.3 | async-start | bytes 2359296 | tf_op jit(solution)/shard_map/all_gather | solution.py:146
  87.7 13.6 %collective-permute-start = (bf16[128,1024]{1,0:T(8,128)(2,1)S(1)}, bf16[128,1024]{1,0:T(8,128)(2,1)S(1)}, u32[]{:S(2)}, u32[]{:S(2)}) collective-permute-start(bf16[128,1024]{1,0:T(8,128)(2,1)S(1)} %all-reduce.1), channel_id=1, source_target_pairs={{0,32},{32,64},{64,96},{96,128},{128,160},{160,192},{192,224},{224... | collective-permute-start | bytes 786440 | tf_op jit(solution)/shard_map/ppermute | solution.py:17
  101.2 19.6 %copy-start.5 = (bf16[128,1024]{1,0:T(8,128)(2,1)}, bf16[128,1024]{1,0:T(8,128)(2,1)S(1)}, u32[]{:S(2)}) copy-start(bf16[128,1024]{1,0:T(8,128)(2,1)S(1)} %collective-permute-done) | copy-start | bytes 786436
  119.4 0.9 copy-start.21
  120.2 90.2 %all-gather.20.cloned.1.call-start = ((), (), s32[]{:S(2)}) async-start(), calls=%async_computation.9 | async-start | bytes 2621440 | tf_op jit(solution)/shard_map/all_gather | solution.py:152
  120.8 1.0 copy-start.7
  120.8 1.7 copy-start.24
  120.9 247.9 %all-gather.24.cloned.1.call-start = ((), (), s32[]{:S(2)}) async-start(), calls=%async_computation.11 | async-start | bytes 20971520 | tf_op jit(solution)/shard_map/all_gather | solution.py:150
  121.4 340.1 %reduce-scatter.4.cloned.1.call-start = ((), (), s32[]{:S(2)}) async-start(), calls=%async_computation.4 | async-start | bytes 2359296 | tf_op jit(solution)/shard_map/reduce_scatter | solution.py:170
  122.5 56.5 %copy-start.17 = (f32[64]{0:T(128)}, f32[64]{0:T(128)S(1)}, u32[]{:S(2)}) copy-start(f32[64]{0:T(128)S(1)} %multiply_exponential_fusion) | copy-start | bytes 772
  122.7 56.4 %copy-start.19 = (f32[128]{0:T(128)}, f32[128]{0:T(128)S(1)}, u32[]{:S(2)}) copy-start(f32[128]{0:T(128)S(1)} %subtract_convert_fusion.2) | copy-start | bytes 1540
  175.7 34.7 %copy-start.1 = (bf16[128,8192]{1,0:T(8,128)(2,1)S(1)}, bf16[128,8192]{1,0:T(8,128)(2,1)}, u32[]{:S(2)}) copy-start(bf16[128,8192]{1,0:T(8,128)(2,1)} %all-gather.14.cloned.1.call-done) | copy-start | bytes 6291460
  376.9 0.7 copy-start.8
  376.9 0.7 copy-start.12
  377.2 1.0 copy-start.6
  377.2 1.0 copy-start.15
  378.0 0.6 copy-start.9
  378.1 0.9 copy-start.13
  378.4 0.9 copy-start.18
  378.4 0.9 copy-start.20
  381.4 13.7 %copy-start.2 = (bf16[1,8192,128]{2,1,0:T(8,128)(2,1)S(1)}, bf16[1,8192,128]{2,1,0:T(8,128)(2,1)}, u32[]{:S(2)}) copy-start(bf16[1,8192,128]{2,1,0:T(8,128)(2,1)} %all-gather.22.cloned.1.call-done) | copy-start | bytes 6291460
  381.4 13.7 %copy-start.11 = (bf16[128,1,64]{0,2,1:T(8,128)(2,1)S(1)}, bf16[128,1,64]{0,2,1:T(8,128)(2,1)}, u32[]{:S(2)}) copy-start(bf16[128,1,64]{0,2,1:T(8,128)(2,1)} %get-tuple-element.19) | copy-start | bytes 49156
  395.1 4.9 copy-start.10
  395.1 4.9 copy-start.14
  405.3 70.6 %copy-start.4 = (bf16[1,1024,1024]{2,1,0:T(8,128)(2,1)S(1)}, bf16[1,1024,1024]{2,1,0:T(8,128)(2,1)}, u32[]{:S(2)}) copy-start(bf16[1,1024,1024]{2,1,0:T(8,128)(2,1)} %all-gather.18.cloned.1.call-done) | copy-start | bytes 6291460
  405.3 70.6 %copy-start.22 = (f32[128]{0:T(128)S(1)}, f32[128]{0:T(128)}, u32[]{:S(2)}) copy-start(f32[128]{0:T(128)} %copy-done.21) | copy-start | bytes 1540
  405.3 70.6 %copy-start.23 = (f32[128]{0:T(128)S(1)}, f32[128]{0:T(128)}, u32[]{:S(2)}) copy-start(f32[128]{0:T(128)} %get-tuple-element.24) | copy-start | bytes 1540
  405.4 130.0 %all-gather.26.cloned.1.call-start = ((), (), s32[]{:S(2)}) async-start(), calls=%async_computation.12 | async-start | bytes 2359296 | tf_op jit(solution)/shard_map/all_gather | solution.py:183
  478.5 91.5 %reduce-scatter.8.cloned.1.call-start = ((), (), s32[]{:S(2)}) async-start(), calls=%async_computation.6 | async-start | bytes 2621440 | tf_op jit(solution)/shard_map/reduce_scatter | solution.py:110
  481.8 122.6 %reduce-scatter.6.cloned.1.call-start = ((), (), s32[]{:S(2)}) async-start(), calls=%async_computation.5 | async-start | bytes 2621440 | tf_op jit(solution)/shard_map/reduce_scatter | solution.py:110
  537.3 11.7 %copy-start.16 = (bf16[128,128,1]{1,0,2:T(8,128)(2,1)S(1)}, bf16[128,128,1]{1,0,2:T(8,128)(2,1)}, u32[]{:S(2)}) copy-start(bf16[128,128,1]{1,0,2:T(8,128)(2,1)} %fusion.44) | copy-start | bytes 98308
  537.3 9.6 %collective-permute-start.1 = (bf16[128,1024]{1,0:T(8,128)(2,1)S(1)}, bf16[128,1024]{1,0:T(8,128)(2,1)S(1)}, u32[]{:S(2)}, u32[]{:S(2)}) collective-permute-start(bf16[128,1024]{1,0:T(8,128)(2,1)S(1)} %reduce_sum.62), channel_id=1, source_target_pairs={{0,224},{32,0},{64,32},{96,64},{128,96},{160,128},{192,160},{224,1... | collective-permute-start | bytes 786440 | tf_op jit(solution)/shard_map/ppermute | solution.py:17
  549.0 1.8 copy-start.3
Sparse Core Ops, SparseCore 0:
  9.8 36.9 all-gather.15
  48.6 33.3 all-gather.17
  83.8 33.3 all-gather.21
  120.4 55.3 all-gather.13
  177.4 32.9 all-gather.19
  212.1 156.6 all-gather.23
  405.5 55.9 reduce-scatter.3
  478.6 56.7 all-gather.25
  537.9 32.0 reduce-scatter.7
  572.4 31.9 reduce-scatter.5
